TPU v7x, 256 devices: a whole 4x4x8 slice. The times are simulated.
256 devices in a mesh: freq: 4 (over x_lo, core), rcv: 64 (over y, x_hi, z).
Axes of the slice: x: 4 (x_hi: 2, x_lo: 2; x = x_hi * 2 + x_lo), y: 4, z: 8, core: 2. Of those that a mesh axis runs over, the one named last changes fastest.
Arguments:
- spectra: bfloat16 [2, 128, 384, 8192], P(None, None, 'freq', 'rcv'), may hold values from -600 to 600
- valid: int32 [384, 8192], P(None, 'rcv'), may hold values from 0 to 1, as said below
- sources: int32 [256], P('rcv'), may hold values from 0 to 8191, as said below
- bounds: int32 [256, 8192, 2], P('freq', 'rcv'), may hold values from 0 to 128, as said below
Outputs:
- lag_corr: bfloat16 [256, 8192, 128], P('freq', 'rcv')
- peak_value: float32 [256, 8192], P('freq', 'rcv')
Inputs may be any that keep to these rules, and one draw needn't show every extreme that they name: `valid`: in each aligned group of 4 sub-windows at most one entry of a channel is 0. Source s is a channel from (s // 4) * 128 to (s // 4 + 1) * 128 - 1; the sources are distinct. bounds[s, c, 0] < bounds[s, c, 1] <= 128, and the window holds 16 to 64 lag samples.
All inputs are finite; a program needn't handle non-finite values.
Results may differ from a plain program's by a relative error of at most 0.007.
Values may be sent and summed in bfloat16 or wider, within the bound.
No kernel may reach another device: no remote copies, remote signals or barrier semaphores. Data moves between devices by JAX's collectives and lax.ppermute only.
A program may use at most 128 MiB of HBM per device.

v0:
```python
import math
import jax
import jax.numpy as jnp
from jax import lax
from jax.sharding import PartitionSpec as P

L = 128


def make_tables(bin_first, bin_count, lag_count, period):
    bins_col = (bin_first + 1 + jnp.arange(bin_count, dtype=jnp.int32))[:, None]
    lag_row = jnp.arange(lag_count, dtype=jnp.int32)[None, :] - lag_count // 2
    phase_int = bins_col * lag_row % period
    angles = phase_int.astype(jnp.float32) * (2.0 * math.pi / period)
    return (jnp.cos(angles).astype(jnp.bfloat16), jnp.sin(angles).astype(jnp.bfloat16))


def local(spectra, valid, sources, bounds):
    freq_index = lax.axis_index("freq")
    rcv_index = lax.axis_index("rcv")
    freq_count = lax.axis_size("freq")
    window_rows = spectra.shape[2]
    channels = valid.shape[1]
    own_valid = lax.dynamic_slice_in_dim(valid, freq_index * window_rows, window_rows, 0).astype(
        jnp.float32
    )
    spectra_f = spectra.astype(jnp.float32)
    energy = jnp.mean(spectra_f[0] * spectra_f[0] + spectra_f[1] * spectra_f[1], axis=0)
    scaling = own_valid / jnp.sqrt(energy + 1e-06)
    whitened = (spectra_f * scaling).astype(jnp.bfloat16)
    regrouped = lax.all_to_all(whitened, "freq", split_axis=1, concat_axis=2, tiled=True)
    bins_dev = regrouped.shape[1]
    offsets = sources - rcv_index * channels
    picked = jnp.take(regrouped, offsets, axis=3)
    valid_half = valid.astype(jnp.bfloat16)
    picked_valid = jnp.take(valid_half, offsets, axis=1)[None, None]
    source_part = lax.all_gather(picked, "rcv", axis=3, tiled=True)
    source_valid = lax.all_gather(picked_valid, "rcv", axis=3, tiled=True)
    part_re = jnp.einsum(
        "fws,fwc->fsc", source_part[0], regrouped[0], preferred_element_type=jnp.float32
    )
    part_re = part_re + jnp.einsum(
        "fws,fwc->fsc", source_part[1], regrouped[1], preferred_element_type=jnp.float32
    )
    part_im = jnp.einsum(
        "fws,fwc->fsc", source_part[0], regrouped[1], preferred_element_type=jnp.float32
    )
    part_im = part_im - jnp.einsum(
        "fws,fwc->fsc", source_part[1], regrouped[0], preferred_element_type=jnp.float32
    )
    counts_part = jnp.einsum(
        "wn,wc->nc", source_valid[0, 0], valid_half, preferred_element_type=jnp.float32
    )
    stack_re = (part_re / counts_part).astype(jnp.bfloat16)
    stack_im = (part_im / counts_part).astype(jnp.bfloat16)
    period = 2 * bins_dev * freq_count
    whole_re, whole_im = (
        lax.all_to_all(stack_re, "freq", split_axis=1, concat_axis=0, tiled=True),
        lax.all_to_all(stack_im, "freq", split_axis=1, concat_axis=0, tiled=True),
    )
    full_cos, full_sin = make_tables(0, bins_dev * freq_count, L, period)
    corr_sum = jnp.einsum(
        "fsc,ft->sct", whole_re, full_cos, preferred_element_type=jnp.float32
    ) - jnp.einsum("fsc,ft->sct", whole_im, full_sin, preferred_element_type=jnp.float32)
    lag_corr = corr_sum.astype(jnp.bfloat16)
    lag_index = jnp.arange(L, dtype=jnp.int32)[None, None, :]
    inside = (lag_index >= bounds[:, :, 0:1]) & (lag_index < bounds[:, :, 1:2])
    peak_value = jnp.max(jnp.where(inside, lag_corr.astype(jnp.float32), -jnp.inf), axis=2)
    return (lag_corr, peak_value)


def solution(mesh):
    in_specs = (P(None, None, "freq", "rcv"), P(None, "rcv"), P("rcv"), P("freq", "rcv", None))
    out_specs = (P("freq", "rcv", None), P("freq", "rcv"))
    return jax.shard_map(local, mesh=mesh, in_specs=in_specs, out_specs=out_specs, check_vma=False)
```

profile of v0, /device:TPU:1, one launch (start us, length us, event | category | flops | bytes accessed | tf_op | source)
XLA Modules:
  0.0 409.4 jit_solution(12215775478795225761)
XLA Ops:
  7.2 4.6 %copy_convert_fusion = f32[2,128,96,128]{3,2,0,1:T(8,128)S(1)} fusion(bf16[2,128,96,128]{3,2,1,0:T(8,128)(2,1)} %param.4), kind=kLoop, calls=%fused_computation.9 | loop fusion | flops 3145728 | bytes 18874368 | tf_op jit(solution)/shard_map/convert_element_type | solution.py:27
  11.7 0.0 copy-start.6
  11.7 0.9 fusion.1
  12.7 0.0 copy-done.6
  12.7 7.2 %multiply_convert_fusion = bf16[2,128,96,128]{3,2,0,1:T(8,128)(2,1)} fusion(f32[96,128]{1,0:T(8,128)S(1)} %rsqrt_multiply_fusion, bf16[2,128,96,128]{3,2,1,0:T(8,128)(2,1)} %param.4), kind=kLoop, calls=%fused_computation.2 | loop fusion | flops 9437184 | bytes 12632064 | tf_op jit(solution)/shard_map/convert_element_type | solution.py:30
  20.0 0.0 copy-start.8
  20.0 8.6 %all-to-all-start = ((bf16[2,128,96,128]{3,2,0,1:T(8,128)(2,1)}), bf16[2,128,96,128]{3,2,0,1:T(8,128)(2,1)}, u32[]{:S(2)}, u32[]{:S(2)}) async-start(bf16[2,128,96,128]{3,2,0,1:T(8,128)(2,1)} %multiply_convert_fusion), calls=%async_computation | async-start | bytes 12582912 | tf_op jit(solution)/shard_map/all_to_all | solution.py:31
  28.6 0.0 all-gather.2.cloned.1.call-start
  28.6 0.0 copy-done.8
  28.6 69.9 %all-to-all-done = bf16[2,128,96,128]{3,2,0,1:T(8,128)(2,1)} async-done(((bf16[2,128,96,128]{3,2,0,1:T(8,128)(2,1)}), bf16[2,128,96,128]{3,2,0,1:T(8,128)(2,1)}, u32[]{:S(2)}, u32[]{:S(2)}) %all-to-all-start) | async-done | bytes 6291488 | tf_op jit(solution)/shard_map/all_to_all | solution.py:31
  98.4 7.4 %copy.50 = bf16[2,32,4,96,128]{4,3,2,1,0:T(8,128)(2,1)} copy(bf16[2,32,4,96,128]{4,3,0,1,2:T(8,128)(2,1)} %bitcast.2) | data formatting | bytes 12582912 | tf_op jit(solution)/shard_map/all_to_all | solution.py:31
  105.8 9.0 %copy.51 = bf16[2,32,384,128]{2,1,0,3:T(8,128)(2,1)} copy(bf16[2,32,384,128]{3,2,1,0:T(8,128)(2,1)} %bitcast.54) | data formatting | bytes 12582912 | tf_op jit(solution)/shard_map/all_to_all | solution.py:31
  114.9 3.4 gather_fusion
  118.3 0.8 select_bitcast_fusion
  119.0 0.0 all-gather.2.cloned.1.call-update
  119.1 0.1 copy.56
  119.2 0.6 gather_fusion.1
  119.8 0.1 bitcast_select_fusion
  119.9 159.3 %all_gather.7 = bf16[1,1,384,256]{2,1,0,3:T(2,128)(2,1)S(1)} all-gather(bf16[1,1,384,4]{2,1,0,3:T(2,128)(2,1)S(1)} %copy.57), channel_id=1, replica_groups=mesh['freq'=4,'rcv'=64] {'rcv'}, dimensions={3}, use_global_device_ids=true | all-gather | bytes 199680 | tf_op jit(solution)/shard_map/all_gather | solution.py:38
  279.2 0.4 copy.58
  279.6 0.2 fusion.7
  279.8 4.0 copy.49
  283.8 1.4 fusion.28
  285.2 0.4 copy.53
  285.6 0.0 copy-start.3
  285.6 2.3 copy.55
  287.9 12.9 %all-gather.2.cloned.1.call-done = bf16[2,32,384,256]{2,1,0,3:T(8,128)(2,1)} async-done(((bf16[2,32,384,4]{2,1,0,3:T(8,128)(2,1)}), bf16[2,32,384,256]{2,1,0,3:T(8,128)(2,1)}) %all-gather.2.cloned.1.call-update) | async-done | bytes 12582928 | tf_op jit(solution)/shard_map/all_gather | solution.py:37
  300.8 6.3 %fusion.27 = (bf16[1,32,384,256]{2,1,0,3:T(8,128)(2,1)S(1)}, bf16[1,32,384,256]{2,1,0,3:T(8,128)(2,1)S(1)}) fusion(bf16[2,32,384,256]{2,1,0,3:T(8,128)(2,1)} %all-gather.2.cloned.1.call-done), kind=kLoop, calls=%fused_computation.52 | loop fusion | bytes 25165824 | tf_op jit(solution)/shard_map/slice | solution.py:43
  307.2 0.0 copy-start.2
  307.2 0.0 copy-start.1
  307.2 0.0 copy-done.3
  307.2 0.0 copy-start.5
  307.2 4.3 %fusion.3 = f32[32,256,128]{2,1,0:T(8,128)S(1)} fusion(bf16[32,384,128]{2,1,0:T(8,128)(2,1)S(1)} %bitcast.57, bf16[1,32,384,256]{2,1,0,3:T(8,128)(2,1)S(1)} %get-tuple-element.17), kind=kOutput, calls=%fused_computation.11 | convolution fusion | flops 805306368 | bytes 13631488 | tf_op jit(solution)/shard_map/fws,fwc->fsc/dot_general | solution.py:39
  311.5 0.0 copy-done.2
  311.5 0.8 copy-done.1
  312.3 0.0 copy-done.5
  312.3 4.5 %divide_convert_fusion.1 = bf16[32,256,128]{2,1,0:T(8,128)(2,1)S(1)} fusion(f32[32,256,128]{2,1,0:T(8,128)S(1)} %fusion.3, f32[256,128]{1,0:T(8,128)S(1)} %fusion.7, bf16[32,384,128]{2,1,0:T(8,128)(2,1)S(1)} %bitcast.60, bf16[1,32,384,256]{2,1,0,3:T(8,128)(2,1)S(1)} %get-tuple-element.16), kind=kOutput, calls=%fused_computation.19 | convolution fusion | flops 808452096 | bytes 15859712 | tf_op jit(solution)/shard_map/fws,fwc->fsc/dot_general | solution.py:42
  316.8 2.7 copy.59
  319.5 19.4 %all-to-all-start.1 = ((bf16[32,256,128]{2,0,1:T(8,128)(2,1)}), bf16[32,256,128]{2,0,1:T(8,128)(2,1)S(1)}, u32[]{:S(2)}, u32[]{:S(2)}) async-start(bf16[32,256,128]{2,0,1:T(8,128)(2,1)} %copy.59), calls=%async_computation.1 | async-start | bytes 4194304 | tf_op jit(solution)/shard_map/all_to_all | solution.py:58
  338.9 0.0 copy-start.4
  338.9 7.9 %fusion.2 = f32[32,256,128]{2,1,0:T(8,128)S(1)} fusion(bf16[32,384,128]{2,1,0:T(8,128)(2,1)} %bitcast.59, bf16[1,32,384,256]{2,1,0,3:T(8,128)(2,1)} %copy-done.2), kind=kOutput, calls=%fused_computation.10 | convolution fusion | flops 805306368 | bytes 13631488 | tf_op jit(solution)/shard_map/fws,fwc->fsc/dot_general | solution.py:45
  346.8 0.0 copy-done.4
  346.8 7.6 %divide_convert_fusion = bf16[32,256,128]{2,1,0:T(8,128)(2,1)S(1)} fusion(f32[32,256,128]{2,1,0:T(8,128)S(1)} %fusion.2, f32[256,128]{1,0:T(8,128)S(1)} %fusion.7, bf16[32,384,128]{2,1,0:T(8,128)(2,1)S(1)} %bitcast.58, bf16[1,32,384,256]{2,1,0,3:T(8,128)(2,1)} %copy-done.1), kind=kOutput, calls=%fused_computation.18 | convolution fusion | flops 808452096 | bytes 15859712 | tf_op jit(solution)/shard_map/fws,fwc->fsc/dot_general | solution.py:48
  354.4 0.0 copy-start.7
  354.4 2.7 copy.61
  357.1 6.6 %all-to-all-done.1 = bf16[32,256,128]{2,0,1:T(8,128)(2,1)S(1)} async-done(((bf16[32,256,128]{2,0,1:T(8,128)(2,1)}), bf16[32,256,128]{2,0,1:T(8,128)(2,1)S(1)}, u32[]{:S(2)}, u32[]{:S(2)}) %all-to-all-start.1) | async-done | bytes 2097184 | tf_op jit(solution)/shard_map/all_to_all | solution.py:58
  363.7 5.3 %all-to-all-start.2 = ((bf16[32,256,128]{2,0,1:T(8,128)(2,1)}), bf16[32,256,128]{2,0,1:T(8,128)(2,1)}, u32[]{:S(2)}, u32[]{:S(2)}) async-start(bf16[32,256,128]{2,0,1:T(8,128)(2,1)} %copy.61), calls=%async_computation.2 | async-start | bytes 4194304 | tf_op jit(solution)/shard_map/all_to_all | solution.py:59
  369.0 0.0 copy-done.7
  369.0 0.1 fusion.29
  369.1 2.0 copy.60
  371.0 0.0 copy-start
  371.0 22.9 %all-to-all-done.2 = bf16[32,256,128]{2,0,1:T(8,128)(2,1)} async-done(((bf16[32,256,128]{2,0,1:T(8,128)(2,1)}), bf16[32,256,128]{2,0,1:T(8,128)(2,1)}, u32[]{:S(2)}, u32[]{:S(2)}) %all-to-all-start.2) | async-done | bytes 2097184 | tf_op jit(solution)/shard_map/all_to_all | solution.py:59
  393.9 2.2 copy.62
  396.1 0.0 copy-done
  396.1 1.0 fusion.13
  397.1 2.5 select_reduce_fusion
  399.6 2.9 copy.63
  (6 shorter events, 0.1 us)
Async XLA Ops:
  11.7 1.0 copy-start.6
  20.0 8.6 %copy-start.8 = (s32[4]{0:T(128)S(1)}, s32[4]{0:T(128)}, u32[]{:S(2)}) copy-start(s32[4]{0:T(128)} %param.6) | copy-start | bytes 52
  20.0 78.5 %all-to-all-start = ((bf16[2,128,96,128]{3,2,0,1:T(8,128)(2,1)}), bf16[2,128,96,128]{3,2,0,1:T(8,128)(2,1)}, u32[]{:S(2)}, u32[]{:S(2)}) async-start(bf16[2,128,96,128]{3,2,0,1:T(8,128)(2,1)} %multiply_convert_fusion), calls=%async_computation | async-start | bytes 12582912 | tf_op jit(solution)/shard_map/all_to_all | solution.py:31
  28.6 272.3 %all-gather.2.cloned.1.call-start = ((), (), s32[]{:S(2)}) async-start(), calls=%async_computation.3 | async-start | bytes 12779520 | tf_op jit(solution)/shard_map/all_gather | solution.py:37
  285.6 21.6 %copy-start.3 = (bf16[1,32,4,96,128]{4,3,2,1,0:T(8,128)(2,1)}, bf16[1,32,4,96,128]{4,3,2,1,0:T(8,128)(2,1)S(1)}, u32[]{:S(2)}) copy-start(bf16[1,32,4,96,128]{4,3,2,1,0:T(8,128)(2,1)S(1)} %copy.53) | copy-start | bytes 9437188
  307.2 4.4 %copy-start.2 = (bf16[1,32,384,256]{2,1,0,3:T(8,128)(2,1)}, bf16[1,32,384,256]{2,1,0,3:T(8,128)(2,1)S(1)}, u32[]{:S(2)}) copy-start(bf16[1,32,384,256]{2,1,0,3:T(8,128)(2,1)S(1)} %get-tuple-element.17) | copy-start | bytes 18874372
  307.2 5.1 %copy-start.1 = (bf16[1,32,384,256]{2,1,0,3:T(8,128)(2,1)}, bf16[1,32,384,256]{2,1,0,3:T(8,128)(2,1)S(1)}, u32[]{:S(2)}) copy-start(bf16[1,32,384,256]{2,1,0,3:T(8,128)(2,1)S(1)} %get-tuple-element.16) | copy-start | bytes 18874372
  307.2 5.1 %copy-start.5 = (bf16[1,32,4,96,128]{4,3,2,1,0:T(8,128)(2,1)S(1)}, bf16[1,32,4,96,128]{4,3,2,1,0:T(8,128)(2,1)}, u32[]{:S(2)}) copy-start(bf16[1,32,4,96,128]{4,3,2,1,0:T(8,128)(2,1)} %copy.55) | copy-start | bytes 9437188
  319.5 44.2 %all-to-all-start.1 = ((bf16[32,256,128]{2,0,1:T(8,128)(2,1)}), bf16[32,256,128]{2,0,1:T(8,128)(2,1)S(1)}, u32[]{:S(2)}, u32[]{:S(2)}) async-start(bf16[32,256,128]{2,0,1:T(8,128)(2,1)} %copy.59), calls=%async_computation.1 | async-start | bytes 4194304 | tf_op jit(solution)/shard_map/all_to_all | solution.py:58
  338.9 7.9 %copy-start.4 = (bf16[1,32,4,96,128]{4,3,2,1,0:T(8,128)(2,1)S(1)}, bf16[1,32,4,96,128]{4,3,2,1,0:T(8,128)(2,1)}, u32[]{:S(2)}) copy-start(bf16[1,32,4,96,128]{4,3,2,1,0:T(8,128)(2,1)} %copy-done.3) | copy-start | bytes 9437188
  354.4 14.6 %copy-start.7 = (s32[64,128,2]{1,2,0:T(2,128)S(1)}, s32[64,128,2]{1,2,0:T(2,128)}, u32[]{:S(2)}) copy-start(s32[64,128,2]{1,2,0:T(2,128)} %param.7) | copy-start | bytes 196612
  363.7 30.2 %all-to-all-start.2 = ((bf16[32,256,128]{2,0,1:T(8,128)(2,1)}), bf16[32,256,128]{2,0,1:T(8,128)(2,1)}, u32[]{:S(2)}, u32[]{:S(2)}) async-start(bf16[32,256,128]{2,0,1:T(8,128)(2,1)} %copy.61), calls=%async_computation.2 | async-start | bytes 4194304 | tf_op jit(solution)/shard_map/all_to_all | solution.py:59
  371.0 25.1 %copy-start = (bf16[32,4,64,128]{3,0,1,2:T(8,128)(2,1)S(1)}, bf16[32,4,64,128]{3,0,1,2:T(8,128)(2,1)}, u32[]{:S(2)}) copy-start(bf16[32,4,64,128]{3,0,1,2:T(8,128)(2,1)} %copy.60) | copy-start | bytes 6291460
Sparse Core Ops, SparseCore 0:
  119.2 181.6 all-gather.1
where the time goes:
time: 410 us; the launch traced here: 409 us
  blocking collectives  159 us (39%)
  waiting for transfers between devices  112 us (27%)
  local copies, waits for them, and re-layouts  48.6 us (12%)
  starting transfers between devices  33.3 us (8%)
  matrix products  28 us (7%)
  between operations  14.3 us (3%)
  other arithmetic  13.6 us (3%)
    all_gather x1, blocking collectives, local(): source_valid = lax.all_gather(picked_valid, 'rcv', axis=3, tiled=True)  159 us
    all_to_all x1, waiting for transfers between devices, local(): lax.all_to_all(whitened, 'freq', split_axis=1, concat_axis=2, tiled=True)  69.9 us
    all_to_all x1, waiting for transfers between devices, local(): lax.all_to_all(stack_im, 'freq', split_axis=1, concat_axis=0, tiled=True)  22.9 us
    all_to_all x3, local copies, waits for them, and re-layouts, local(): lax.all_to_all(whitened, 'freq', split_axis=1, concat_axis=2, tiled=True)  20.4 us
    all_to_all x1, starting transfers between devices, local(): lax.all_to_all(stack_re, 'freq', split_axis=1, concat_axis=0, tiled=True)  19.4 us
    all_gather x1, waiting for transfers between devices, local(): source_part = lax.all_gather(picked, 'rcv', axis=3, tiled=True)  12.9 us
    all_to_all x1, starting transfers between devices, local(): lax.all_to_all(whitened, 'freq', split_axis=1, concat_axis=2, tiled=True)  8.59 us
  transfers between devices with their start and end apart: 4, of which 4 were waited for; matrix products, arithmetic and copies ran while one was open for 7% of the time, Pallas kernels for 0%

commit v1 on v0

--- a/solution.py
+++ b/solution.py
@@ -34,7 +34,9 @@
     picked = jnp.take(regrouped, offsets, axis=3)
     valid_half = valid.astype(jnp.bfloat16)
     picked_valid = jnp.take(valid_half, offsets, axis=1)[None, None]
-    source_part = lax.all_gather(picked, "rcv", axis=3, tiled=True)
+    source_part = jnp.concatenate(
+        lax.all_to_all(jnp.stack([picked] * lax.axis_size("rcv")), "rcv", 0, 0), axis=3
+    )
     source_valid = lax.all_gather(picked_valid, "rcv", axis=3, tiled=True)
     part_re = jnp.einsum(
         "fws,fwc->fsc", source_part[0], regrouped[0], preferred_element_type=jnp.float32

time: 410 us -> 719 us (1.75)
  blocking collectives: 159 us -> 421 us
  local copies, waits for them, and re-layouts: 48.6 us -> 99.8 us
  starting transfers between devices: 33.3 us -> 59.1 us
  between operations: 14.3 us -> 0.82 us
  waiting for transfers between devices: 112 us -> 103 us
  matrix products: 28 us -> 20.4 us
    all_gather x1, blocking collectives: 159 us -> 421 us  [local(): source_valid = lax.all_gather(picked_valid, 'rcv', axis=3, tiled=True)]
    squeeze x0 -> x2, local copies, waits for them, and re-layouts: none -> 21.6 us  [the longest x1 10.9 us: local(): source_part[1]]
    all_to_all x1, starting transfers between devices: 19.4 us -> 33.3 us  [local(): lax.all_to_all(stack_re, 'freq', split_axis=1, concat_axis=0, tiled=True)]
    slice x1 -> x2, local copies, waits for them, and re-layouts: 6.33 us -> 20 us  [local(): source_part[1]]
    all_gather x1 -> x0, waiting for transfers between devices: 12.9 us -> none  [local(): source_part = lax.all_gather(picked, 'rcv', axis=3, tiled=True)]
    all_to_all x0 -> x1, starting transfers between devices: none -> 12.8 us  [local(): lax.all_to_all(jnp.stack([picked] * lax.axis_size('rcv')), 'rcv', 0, 0)]
    another operation x0 -> x1, local copies, waits for them, and re-layouts: none -> 7.32 us  [local(): jnp.stack([picked] * lax.axis_size('rcv'))]
  transfers between devices with their start and end apart: 4 -> 4, of which waited for: 4 -> 3; matrix products, arithmetic and copies ran while one was open for 7% -> 4% of each run, Pallas kernels for 0% -> 0%
where the time goes in v1:
time: 719 us; the launch traced here: 717 us
  blocking collectives  421 us (59%)
  waiting for transfers between devices  103 us (14%)
  local copies, waits for them, and re-layouts  99.8 us (14%)
  starting transfers between devices  59.1 us (8%)
  matrix products  20.4 us (3%)
  other arithmetic  13 us (2%)
    all_gather x1, blocking collectives, local(): source_valid = lax.all_gather(picked_valid, 'rcv', axis=3, tiled=True)  421 us
    all_to_all x1, waiting for transfers between devices, local(): lax.all_to_all(whitened, 'freq', split_axis=1, concat_axis=2, tiled=True)  69.9 us
    all_to_all x1, starting transfers between devices, local(): lax.all_to_all(stack_re, 'freq', split_axis=1, concat_axis=0, tiled=True)  33.3 us
    all_to_all x1, waiting for transfers between devices, local(): lax.all_to_all(stack_im, 'freq', split_axis=1, concat_axis=0, tiled=True)  21.2 us
    all_to_all x3, local copies, waits for them, and re-layouts, local(): lax.all_to_all(whitened, 'freq', split_axis=1, concat_axis=2, tiled=True)  20.4 us
    slice x2, local copies, waits for them, and re-layouts, local(): source_part[1]  20 us
  transfers between devices with their start and end apart: 4, of which 3 were waited for; matrix products, arithmetic and copies ran while one was open for 4% of the time, Pallas kernels for 0%

profile of v1, /device:TPU:1, one launch (start us, length us, event | category | flops | bytes accessed | tf_op | source)
XLA Modules:
  0.0 717.2 jit_solution(11337690449416650101)
XLA Ops:
  0.6 4.6 copy_convert_fusion
  5.2 0.0 copy-start.4
  5.2 0.9 fusion.1
  6.2 0.0 copy-done.4
  6.2 7.2 %multiply_convert_fusion = bf16[2,128,96,128]{3,2,0,1:T(8,128)(2,1)} fusion(f32[96,128]{1,0:T(8,128)S(1)} %rsqrt_multiply_fusion, bf16[2,128,96,128]{3,2,1,0:T(8,128)(2,1)} %param.4), kind=kLoop, calls=%fused_computation.2 | loop fusion | flops 9437184 | bytes 12632064 | tf_op jit(solution)/shard_map/convert_element_type | solution.py:30
  13.4 0.0 copy-start.6
  13.4 8.6 %all-to-all-start = ((bf16[2,128,96,128]{3,2,0,1:T(8,128)(2,1)}), bf16[2,128,96,128]{3,2,0,1:T(8,128)(2,1)}, u32[]{:S(2)}, u32[]{:S(2)}) async-start(bf16[2,128,96,128]{3,2,0,1:T(8,128)(2,1)} %multiply_convert_fusion), calls=%async_computation | async-start | bytes 12582912 | tf_op jit(solution)/shard_map/all_to_all | solution.py:31
  22.1 0.0 copy-done.6
  22.1 69.9 %all-to-all-done = bf16[2,128,96,128]{3,2,0,1:T(8,128)(2,1)} async-done(((bf16[2,128,96,128]{3,2,0,1:T(8,128)(2,1)}), bf16[2,128,96,128]{3,2,0,1:T(8,128)(2,1)}, u32[]{:S(2)}, u32[]{:S(2)}) %all-to-all-start) | async-done | bytes 6291488 | tf_op jit(solution)/shard_map/all_to_all | solution.py:31
  91.9 7.4 %copy.52 = bf16[2,32,4,96,128]{4,3,2,1,0:T(8,128)(2,1)} copy(bf16[2,32,4,96,128]{4,3,0,1,2:T(8,128)(2,1)} %bitcast.2) | data formatting | bytes 12582912 | tf_op jit(solution)/shard_map/all_to_all | solution.py:31
  99.3 9.1 %copy.53 = bf16[2,32,384,128]{2,1,0,3:T(8,128)(2,1)} copy(bf16[2,32,384,128]{3,2,1,0:T(8,128)(2,1)} %bitcast.51) | data formatting | bytes 12582912 | tf_op jit(solution)/shard_map/all_to_all | solution.py:31
  108.4 3.4 gather_fusion
  111.8 0.1 select_bitcast_fusion
  111.9 0.2 copy.54
  112.0 7.3 %stack.2 = bf16[64,2,32,384,4]{3,4,2,1,0:T(4,128)(2,1)} broadcast(bf16[2,32,384,4]{2,3,1,0:T(4,128)(2,1)S(1)} %copy.54), dimensions={1,2,3,4} | broadcast | bytes 12779520 | tf_op jit(solution)/shard_map/stack | solution.py:38
  119.3 12.8 %all-to-all-start.1 = ((bf16[64,2,32,384,4]{3,4,2,1,0:T(4,128)(2,1)}), bf16[64,2,32,384,4]{3,4,2,1,0:T(4,128)(2,1)}, u32[]{:S(2)}, u32[]{:S(2)}) async-start(bf16[64,2,32,384,4]{3,4,2,1,0:T(4,128)(2,1)} %stack.2), calls=%async_computation.1 | async-start | bytes 25165824 | tf_op jit(solution)/shard_map/all_to_all | solution.py:38
  132.1 0.1 copy.59
  132.3 0.6 gather_fusion.1
  132.9 0.1 bitcast_select_fusion
  132.9 420.9 %all_gather.3 = bf16[1,1,384,256]{2,1,0,3:T(2,128)(2,1)S(1)} all-gather(bf16[1,1,384,4]{2,1,0,3:T(2,128)(2,1)S(1)} %copy.60), channel_id=1, replica_groups=mesh['freq'=4,'rcv'=64] {'rcv'}, dimensions={3}, use_global_device_ids=true | all-gather | bytes 199680 | tf_op jit(solution)/shard_map/all_gather | solution.py:40
  553.9 0.4 copy.61
  554.3 0.2 fusion.3
  554.5 3.9 copy.51
  558.5 1.4 fusion.24
  559.9 2.1 copy.56
  562.0 2.1 copy.58
  564.1 0.0 all-to-all-done.1
  564.1 11.3 %fusion.23 = (bf16[1,32,384,64,4]{2,4,1,0,3:T(4,128)(2,1)}, bf16[1,32,384,64,4]{2,4,1,0,3:T(4,128)(2,1)S(1)}) fusion(bf16[2,32,384,64,4]{2,4,1,0,3:T(4,128)(2,1)} %bitcast.5), kind=kLoop, calls=%fused_computation.46 | loop fusion | bytes 25165824 | tf_op jit(solution)/shard_map/slice | solution.py:45
  575.5 6.0 copy.55
  581.4 10.7 %squeeze.10 = bf16[32,384,256]{1,2,0:T(8,128)(2,1)} reshape(bf16[1,32,384,64,4]{2,4,3,1,0:T(4,128)(2,1)} %copy.55) | data formatting | bytes 12582912 | tf_op jit(solution)/shard_map/squeeze | solution.py:42
  592.2 8.6 %copy.57 = bf16[1,32,384,64,4]{2,4,3,1,0:T(4,128)(2,1)} copy(bf16[1,32,384,64,4]{2,4,1,0,3:T(4,128)(2,1)} %get-tuple-element.16) | data formatting | bytes 12582912 | tf_op jit(solution)/shard_map/slice | solution.py:45
  600.8 0.0 copy-start
  600.8 10.9 %squeeze.12 = bf16[32,384,256]{1,2,0:T(8,128)(2,1)} reshape(bf16[1,32,384,64,4]{2,4,3,1,0:T(4,128)(2,1)} %copy.57) | data formatting | bytes 12582912 | tf_op jit(solution)/shard_map/squeeze | solution.py:45
  611.7 0.0 copy-done
  611.7 0.0 copy-start.1
  611.7 0.0 copy-start.3
  611.7 4.7 fusion.26
  616.4 0.0 copy-done.1
  616.4 0.8 copy-done.3
  617.2 1.8 divide_convert_fusion.1
  619.0 2.7 copy.62
  621.7 33.3 %all-to-all-start.2 = ((bf16[32,256,128]{2,0,1:T(8,128)(2,1)}), bf16[32,256,128]{2,0,1:T(8,128)(2,1)}, u32[]{:S(2)}, u32[]{:S(2)}) async-start(bf16[32,256,128]{2,0,1:T(8,128)(2,1)} %copy.62), calls=%async_computation.2 | async-start | bytes 4194304 | tf_op jit(solution)/shard_map/all_to_all | solution.py:60
  655.0 5.5 fusion.27
  660.5 4.6 divide_convert_fusion
  665.1 0.0 copy-start.5
  665.1 2.7 copy.64
  667.8 12.2 %all-to-all-done.2 = bf16[32,256,128]{2,0,1:T(8,128)(2,1)} async-done(((bf16[32,256,128]{2,0,1:T(8,128)(2,1)}), bf16[32,256,128]{2,0,1:T(8,128)(2,1)}, u32[]{:S(2)}, u32[]{:S(2)}) %all-to-all-start.2) | async-done | bytes 2097184 | tf_op jit(solution)/shard_map/all_to_all | solution.py:60
  679.9 4.4 all-to-all-start.3
  684.4 0.0 copy-done.5
  684.4 0.1 fusion.25
  684.4 3.6 copy.63
  688.0 21.2 %all-to-all-done.3 = bf16[32,256,128]{2,0,1:T(8,128)(2,1)S(1)} async-done(((bf16[32,256,128]{2,0,1:T(8,128)(2,1)}), bf16[32,256,128]{2,0,1:T(8,128)(2,1)S(1)}, u32[]{:S(2)}, u32[]{:S(2)}) %all-to-all-start.3) | async-done | bytes 2097184 | tf_op jit(solution)/shard_map/all_to_all | solution.py:61
  709.2 0.0 copy-start.2
  709.2 0.6 copy.65
  709.8 0.9 copy-done.2
  710.8 1.0 fusion.9
  711.8 2.6 select_reduce_fusion
  714.3 2.9 copy.66
  (6 shorter events, 0.1 us)
Async XLA Ops:
  5.2 1.0 copy-start.4
  13.4 8.6 %copy-start.6 = (s32[4]{0:T(128)S(1)}, s32[4]{0:T(128)}, u32[]{:S(2)}) copy-start(s32[4]{0:T(128)} %param.6) | copy-start | bytes 52
  13.4 78.5 %all-to-all-start = ((bf16[2,128,96,128]{3,2,0,1:T(8,128)(2,1)}), bf16[2,128,96,128]{3,2,0,1:T(8,128)(2,1)}, u32[]{:S(2)}, u32[]{:S(2)}) async-start(bf16[2,128,96,128]{3,2,0,1:T(8,128)(2,1)} %multiply_convert_fusion), calls=%async_computation | async-start | bytes 12582912 | tf_op jit(solution)/shard_map/all_to_all | solution.py:31
  119.3 444.8 %all-to-all-start.1 = ((bf16[64,2,32,384,4]{3,4,2,1,0:T(4,128)(2,1)}), bf16[64,2,32,384,4]{3,4,2,1,0:T(4,128)(2,1)}, u32[]{:S(2)}, u32[]{:S(2)}) async-start(bf16[64,2,32,384,4]{3,4,2,1,0:T(4,128)(2,1)} %stack.2), calls=%async_computation.1 | async-start | bytes 25165824 | tf_op jit(solution)/shard_map/all_to_all | solution.py:38
  600.8 10.9 %copy-start = (bf16[1,32,4,96,128]{4,3,2,1,0:T(8,128)(2,1)S(1)}, bf16[1,32,4,96,128]{4,3,2,1,0:T(8,128)(2,1)}, u32[]{:S(2)}) copy-start(bf16[1,32,4,96,128]{4,3,2,1,0:T(8,128)(2,1)} %copy.56) | copy-start | bytes 9437188
  611.7 4.7 copy-start.1
  611.7 5.6 copy-start.3
  621.7 58.2 %all-to-all-start.2 = ((bf16[32,256,128]{2,0,1:T(8,128)(2,1)}), bf16[32,256,128]{2,0,1:T(8,128)(2,1)}, u32[]{:S(2)}, u32[]{:S(2)}) async-start(bf16[32,256,128]{2,0,1:T(8,128)(2,1)} %copy.62), calls=%async_computation.2 | async-start | bytes 4194304 | tf_op jit(solution)/shard_map/all_to_all | solution.py:60
  665.1 19.3 %copy-start.5 = (s32[64,128,2]{1,2,0:T(2,128)S(1)}, s32[64,128,2]{1,2,0:T(2,128)}, u32[]{:S(2)}) copy-start(s32[64,128,2]{1,2,0:T(2,128)} %param.7) | copy-start | bytes 196612
  679.9 29.3 %all-to-all-start.3 = ((bf16[32,256,128]{2,0,1:T(8,128)(2,1)}), bf16[32,256,128]{2,0,1:T(8,128)(2,1)S(1)}, u32[]{:S(2)}, u32[]{:S(2)}) async-start(bf16[32,256,128]{2,0,1:T(8,128)(2,1)} %copy.64), calls=%async_computation.3 | async-start | bytes 4194304 | tf_op jit(solution)/shard_map/all_to_all | solution.py:61
  709.2 1.6 copy-start.2
